TPU v7x, 32 devices: a whole 2x2x4 slice. The times are simulated.
32 devices in a mesh: grp: 2 (over x), chan: 16 (over z, y, core).
Axes of the slice: x: 2, y: 2, z: 4, core: 2. Of those that a mesh axis runs over, the one named last changes fastest.
Arguments:
- voltages: bfloat16 [2, 1024, 2, 32, 512], P(None, 'chan', None, None, 'grp'), parts along dimension 4, may hold values from -80 to 80
- gains: float32 [2, 2, 1024], P(None, None, 'chan'), may hold values from -1 to 1
- feed_cyl: int32 [1024], replicated, may hold values from 0 to 3, as said below
- feed_ns: int32 [1024], replicated, may hold values from 0 to 255
- ew_index: int32 [4, 4], replicated, may hold values from 0 to 63
- ns_beam: int32 [256], replicated, may hold values from 0 to 511
Outputs:
- intensity: float32 [1024, 8, 512], P('chan', 'grp'), parts along dimension 1
There are 2 independent parts, one for each index of `grp`. A program takes and returns all parts, laid end to end along the dimension named above; an argument that names none is the same for every part. Nothing has to cross between parts.
Inputs may be any that keep to these rules, and one draw needn't show every extreme that they name: Together, feed_cyl and feed_ns name every pair of a cylinder and a north-south position exactly once.
All inputs are finite; a program needn't handle non-finite values.
Results may differ from a plain program's by a relative error of at most 0.0018.
Values may be sent and summed in bfloat16 or wider, within the bound.
A program may use at most 128 MiB of HBM per device.

v0:
```python
import math

import jax
import jax.numpy as jnp
from jax import lax
from jax.sharding import PartitionSpec as P

CYL = 4
NSF = 256
EWB = 4
NSB = 256
EW_PH = 64
UP = 16
DS = 4
FEEDS = 1024
BEAMS = 1024
TOUT = 4


eps_power = 1e-06


def phase_table(feed_cyl, feed_ns, ew_index, ns_beam):
    modulus = 2 * NSF * EW_PH
    cyl_onehot = (feed_cyl[:, None] == jnp.arange(CYL, dtype=jnp.int32)[None, :]).astype(jnp.int32)
    ew_term = jnp.sum(cyl_onehot[:, None, :] * ew_index[None, :, :], axis=2)
    ns_term = feed_ns[:, None] * ns_beam[None, :] * EW_PH
    steps_int = (ew_term[:, :, None] * (2 * NSF) + ns_term[:, None, :]) % modulus
    angles = steps_int.reshape(FEEDS, EWB * NSB).astype(jnp.float32) * (2.0 * math.pi / modulus)
    cosine = jnp.cos(angles).astype(jnp.bfloat16)
    sine_part = jnp.sin(angles).astype(jnp.bfloat16)
    upper_rows = jnp.concatenate([cosine, sine_part], axis=1)
    lower_rows = jnp.concatenate([-sine_part, cosine], axis=1)
    return jnp.concatenate([upper_rows, lower_rows], axis=0)


def upchannel_table():
    bin_index = jnp.arange(UP, dtype=jnp.int32)
    angles = (bin_index[:, None] * bin_index[None, :] % UP).astype(jnp.float32) * (
        2.0 * math.pi / UP
    )
    cosine = jnp.cos(angles)
    sine_part = jnp.sin(angles)
    return jnp.stack([jnp.stack([cosine, -sine_part], -1), jnp.stack([sine_part, cosine], -1)], 1)


def shards(voltages, gains, feed_cyl, feed_ns, ew_index, ns_beam):
    weights = phase_table(feed_cyl, feed_ns, ew_index, ns_beam).reshape(2, FEEDS, 2 * BEAMS)
    fine_table = upchannel_table()
    sample = voltages.astype(jnp.float32)
    gain_real = gains[0].T[:, :, None, None]
    gain_imag = gains[1].T[:, :, None, None]
    calibrated = jnp.stack(
        [
            (gain_real * sample[0] - gain_imag * sample[1]).astype(jnp.bfloat16),
            (gain_real * sample[1] + gain_imag * sample[0]).astype(jnp.bfloat16),
        ]
    )
    arrived = lax.all_to_all(calibrated, "chan", split_axis=3, concat_axis=1, tiled=True)
    pieces = arrived.shape[2]
    channels = arrived.shape[3]
    beam_sums = jnp.einsum("rfpct,rfq->pctq", arrived, weights, preferred_element_type=jnp.float32)
    beam_sums = beam_sums.reshape(pieces, channels, TOUT, DS, UP, 2, BEAMS)
    fine_bins = jnp.einsum(
        "pcudjrb,jrks->pbudcks", beam_sums, fine_table, precision=lax.Precision.HIGHEST
    )
    beam_power = jnp.sum(jnp.sum(fine_bins * fine_bins, axis=(3, 6)), axis=0)
    total_chans = beam_power.shape[2] * lax.axis_size("chan")
    band_sum = lax.psum(jnp.sum(beam_power, axis=(2, 3)), "chan")
    baseline = band_sum / (total_chans * UP)
    normed = beam_power / (baseline[:, :, None, None] + eps_power)
    intensity = lax.all_to_all(normed, "chan", split_axis=0, concat_axis=2, tiled=True)
    return intensity.reshape(intensity.shape[0], TOUT, intensity.shape[2] * UP)


def solution(mesh):
    placed = (P(None, "chan", None, None, "grp"), P(None, None, "chan"), P(), P(), P(), P())
    return jax.shard_map(
        shards, mesh=mesh, in_specs=placed, out_specs=P("chan", "grp", None), check_vma=False
    )
```

profile of v0, /device:TPU:0, one launch (start us, length us, event | category | flops | bytes accessed | tf_op | source)
XLA Modules:
  0.0 246.4 jit_solution(4950931290050938220)
XLA Ops:
  0.0 0.7 slice_bitcast_fusion.1
  0.7 4.6 %copy_convert_fusion = f32[2,64,2,32,256]{4,1,2,0,3:T(8,128)S(1)} fusion(bf16[2,64,2,32,256]{4,3,2,1,0:T(8,128)(2,1)} %param.6), kind=kLoop, calls=%fused_computation.16 | loop fusion | flops 2097152 | bytes 12582912 | tf_op jit(solution)/shard_map/convert_element_type | solution.py:50
  5.3 1.5 subtract_convert_fusion
  6.8 2.3 pad_maximum_fusion
  9.1 7.6 %all-to-all-start = ((bf16[2,64,2,32,256]{4,1,2,0,3:T(8,128)(2,1)}), bf16[2,64,2,32,256]{4,1,2,0,3:T(8,128)(2,1)}, u32[]{:S(2)}, u32[]{:S(2)}) async-start(bf16[2,64,2,32,256]{4,1,2,0,3:T(8,128)(2,1)} %pad_maximum_fusion), calls=%async_computation | async-start | bytes 8388608 | tf_op jit(solution)/shard_map/all_to_all | solution.py:59
  16.7 0.0 copy-done.1
  16.7 0.1 multiply_reduce_fusion
  16.9 0.2 copy.57
  17.1 0.2 multiply_multiply_fusion
  17.3 3.7 %broadcast_add_fusion = s32[1024,4,256]{2,1,0:T(4,128)S(1)} fusion(s32[1024,256]{1,0:T(8,128)S(1)} %multiply_multiply_fusion, s32[1024,4]{1,0:T(8,128)S(1)} %copy.57), kind=kLoop, calls=%fused_computation.21 | loop fusion | flops 1048576 | bytes 5259264 | tf_op jit(solution)/shard_map/add | solution.py:28
  21.1 1.0 copy.77
  22.1 15.4 %cosine_convert_fusion = bf16[1024,1024]{1,0:T(8,128)(2,1)S(1)} fusion(s32[1024,1024]{1,0:T(8,128)S(1)} %bitcast.60), kind=kLoop, calls=%fused_computation.18 | loop fusion | flops 14680064 | bytes 6291456 | tf_op jit(solution)/shard_map/convert_element_type | solution.py:30
  37.5 15.8 %fusion.23 = (bf16[1024,1024]{1,0:T(8,128)(2,1)S(1)}, bf16[1024,1024]{1,0:T(8,128)(2,1)S(1)}) fusion(s32[1024,1024]{1,0:T(8,128)S(1)} %bitcast.61), kind=kLoop, calls=%fused_computation.49 | loop fusion | flops 17825792 | bytes 8388608 | tf_op jit(solution)/shard_map/neg | solution.py:33
  53.3 36.8 %maximum_maximum_fusion = bf16[2048,2048]{1,0:T(8,128)(2,1)} fusion(bf16[1024,1024]{1,0:T(8,128)(2,1)S(1)} %cosine_convert_fusion, bf16[1024,1024]{1,0:T(8,128)(2,1)S(1)} %get-tuple-element.7, bf16[1024,1024]{1,0:T(8,128)(2,1)S(1)} %get-tuple-element.8), kind=kLoop, calls=%fused_computation | loop fusion | flops 33554432 | bytes 14680064 | tf_op jit(solution)/shard_map/concatenate | solution.py:34
  90.1 11.8 %copy.58 = bf16[2048,1024,2]{1,0,2:T(8,128)(2,1)} copy(bf16[2048,1024,2]{0,1,2:T(8,128)(2,1)} %bitcast.62) | data formatting | bytes 16777216 | tf_op jit(solution)/shard_map/rfpct,rfq->pctq/dot_general | solution.py:62
  102.0 0.1 fusion.21
  102.0 0.1 fusion.19
  102.1 0.0 all-to-all-done
  102.1 4.8 %copy.55 = bf16[2,16,64,2,2,256]{5,2,1,4,3,0:T(8,128)(2,1)} copy(bf16[2,16,64,2,2,256]{5,2,3,0,4,1:T(8,128)(2,1)} %bitcast.11) | data formatting | bytes 8388608 | tf_op jit(solution)/shard_map/all_to_all | solution.py:59
  106.9 6.3 %copy.56 = bf16[2,2,256,1024,2]{3,2,4,1,0:T(8,128)(2,1)} copy(bf16[2,2,256,1024,2]{2,3,1,0,4:T(8,128)(2,1)} %bitcast.65) | data formatting | bytes 8388608 | tf_op jit(solution)/shard_map/rfpct,rfq->pctq/dot_general | solution.py:62
  113.1 12.6 %fusion.2 = f32[2,2,4,4,16,2,1024,1]{6,4,7,5,3,2,1,0:T(8,128)S(1)} fusion(bf16[2,1024,1024,2,1,1,1,1]{2,1,0,3,7,6,5,4:T(8,128)(2,1)} %bitcast.66, bf16[2,2,4,4,16,1024,2,1]{5,4,3,2,6,1,0,7:T(8,128)(2,1)} %bitcast.68), kind=kOutput, calls=%fused_computation.4 | convolution fusion | flops 8589934592 | bytes 20971520 | tf_op jit(solution)/shard_map/rfpct,rfq->pctq/dot_general | solution.py:62
  125.7 8.3 %fusion.4 = (f32[4,1024]{1,0:T(4,128)S(1)}, f32[16,2,4,1024]{3,0,2,1:T(8,128)S(1)}) fusion(f32[2,2,4,4,16,2,1024,1]{6,4,7,5,3,2,1,0:T(8,128)S(1)} %fusion.2, f32[16,1,16,2]{0,2,1,3:T(8,128)S(1)} %get-tuple-element.12, f32[16,1,16,2]{0,2,1,3:T(8,128)S(1)} %get-tuple-element.11), kind=kOutput, calls=%fused_computation.6 | convolution fusion | flops 811463680 | bytes 8933376 | tf_op jit(solution)/shard_map/pcudjrb,jrks->pbudcks/dot_general | solution.py:64
  134.0 67.9 %psum.7 = f32[1024,4]{0,1:T(4,128)S(1)} all-reduce(f32[1024,4]{0,1:T(4,128)S(1)} %bitcast.69), channel_id=1, replica_groups=mesh['grp'=2,'chan'=16] {'chan'}, use_global_device_ids=true, to_apply=%region_3.4 | all-reduce | flops 4096 | bytes 32768 | tf_op jit(solution)/shard_map/psum | solution.py:69
  201.9 0.1 bitcast_divide_fusion
  202.0 4.3 %copy.61 = f32[1024,4,2,16]{3,2,1,0:T(2,128)} copy(f32[1024,4,2,16]{0,3,1,2:T(8,128)S(1)} %bitcast_divide_fusion) | data formatting | bytes 1048576 | tf_op jit(solution)/shard_map/div | solution.py:71
  206.3 7.3 %reshape.151 = f32[16,1,8192]{2,1,0:T(1,128)S(1)} reshape(f32[1024,4,2,16]{3,2,1,0:T(2,128)} %copy.61) | data formatting | bytes 1048576
  213.7 17.1 %all_to_all.33 = f32[16,1,8192]{2,1,0:T(1,128)S(1)} all-to-all(f32[16,1,8192]{2,1,0:T(1,128)S(1)} %reshape.151), channel_id=1, replica_groups=mesh['grp'=2,'chan'=16] {'chan'}, dimensions={0} | all-to-all | bytes 1048576 | tf_op jit(solution)/shard_map/all_to_all | solution.py:72
  230.7 0.5 broadcast.177
  231.2 1.9 reduce.4
  233.1 6.9 %reshape.152 = f32[1024,4,2,16]{3,2,1,0:T(2,128)} reshape(f32[16,8192]{1,0:T(8,128)S(1)} %reduce.4) | data formatting | bytes 1048576
  240.0 5.2 %copy.76 = f32[16,64,4,2,16]{1,4,3,0,2:T(8,128)S(1)} copy(f32[16,64,4,2,16]{4,3,2,1,0:T(2,128)} %bitcast.63) | data formatting | bytes 1048576 | tf_op jit(solution)/shard_map/all_to_all | solution.py:72
  245.2 1.2 copy.64
  (11 shorter events, 0.0 us)
Async XLA Ops:
  9.1 7.6 %copy-start.1 = (s32[1024]{0:T(1024)S(1)}, s32[1024]{0:T(1024)}, u32[]{:S(2)}) copy-start(s32[1024]{0:T(1024)} %param.8) | copy-start | bytes 12292
  9.1 7.6 %copy-start.2 = (s32[4,4]{1,0:T(4,128)S(1)}, s32[4,4]{1,0:T(4,128)}, u32[]{:S(2)}) copy-start(s32[4,4]{1,0:T(4,128)} %param.10) | copy-start | bytes 196
  9.1 8.0 %copy-start = (s32[1024]{0:T(1024)S(1)}, s32[1024]{0:T(1024)}, u32[]{:S(2)}) copy-start(s32[1024]{0:T(1024)} %param.9) | copy-start | bytes 12292
  9.1 8.0 %copy-start.3 = (s32[256]{0:T(256)S(1)}, s32[256]{0:T(256)}, u32[]{:S(2)}) copy-start(s32[256]{0:T(256)} %param.11) | copy-start | bytes 3076
  9.1 93.0 %all-to-all-start = ((bf16[2,64,2,32,256]{4,1,2,0,3:T(8,128)(2,1)}), bf16[2,64,2,32,256]{4,1,2,0,3:T(8,128)(2,1)}, u32[]{:S(2)}, u32[]{:S(2)}) async-start(bf16[2,64,2,32,256]{4,1,2,0,3:T(8,128)(2,1)} %pad_maximum_fusion), calls=%async_computation | async-start | bytes 8388608 | tf_op jit(solution)/shard_map/all_to_all | solution.py:59
where the time goes:
time: 247 us; the launch traced here: 246 us
  blocking collectives  85 us (34%)
  other arithmetic  82.6 us (33%)
  local copies, waits for them, and re-layouts  50.2 us (20%)
  matrix products  20.8 us (8%)
  starting transfers between devices  7.58 us (3%)
    psum x1, blocking collectives, shards(): band_sum = lax.psum(jnp.sum(beam_power, axis=(2, 3)), 'chan')  67.9 us
    concatenate x1, other arithmetic, phase_table(): return jnp.concatenate([upper_rows, lower_rows], axis=0)  36.8 us
    dot_general x2, local copies, waits for them, and re-layouts, shards(): jnp.einsum('rfpct,rfq->pctq', arrived, weights, preferred_element_type=jn...  18.1 us
    all_to_all x1, blocking collectives, shards(): lax.all_to_all(normed, 'chan', split_axis=0, concat_axis=2, tiled=True)  17.1 us
    neg x1, other arithmetic, phase_table(): lower_rows = jnp.concatenate([-sine_part, cosine], axis=1)  15.8 us
    convert_element_type x1, other arithmetic, phase_table(): cosine = jnp.cos(angles).astype(jnp.bfloat16)  15.4 us
    unnamed x11, local copies, waits for them, and re-layouts  15.2 us
    dot_general x1, matrix products, shards(): jnp.einsum('rfpct,rfq->pctq', arrived, weights, preferred_element_type=jn...  12.6 us
  transfers between devices with their start and end apart: 1, of which 0 were waited for; matrix products, arithmetic and copies ran while one was open for 35% of the time, Pallas kernels for 0%

commit v1 on v0

--- a/solution.py
+++ b/solution.py
@@ -1,8 +1,12 @@
+import functools
 import math
 
 import jax
 import jax.numpy as jnp
+import numpy as np
 from jax import lax
+from jax.experimental import pallas as pl
+from jax.experimental.pallas import tpu as pltpu
 from jax.sharding import PartitionSpec as P
 
 CYL = 4
@@ -18,6 +22,7 @@
 
 
 eps_power = 1e-06
+MESH = pl.DeviceIdType.MESH
 
 
 def phase_table(feed_cyl, feed_ns, ew_index, ns_beam):
@@ -72,9 +77,271 @@
     intensity = lax.all_to_all(normed, "chan", split_axis=0, concat_axis=2, tiled=True)
     return intensity.reshape(intensity.shape[0], TOUT, intensity.shape[2] * UP)
 
+def fft(values):
+    size = len(values)
+    if size == 1:
+        return values
+    even = fft(values[0::2])
+    odd = fft(values[1::2])
+    low, high = [], []
+    for k in range(size // 2):
+        er, ei = even[k]
+        xr, xi = odd[k]
+        if k == 0:
+            tr, ti = xr, xi
+        elif 4 * k == size:
+            tr, ti = xi, -xr
+        else:
+            c = math.cos(2.0 * math.pi * k / size)
+            s = math.sin(2.0 * math.pi * k / size)
+            if 8 * k == size:
+                tr, ti = (xr + xi) * c, (xi - xr) * c
+            elif 8 * k == 3 * size:
+                tr, ti = (xi - xr) * s, -(xr + xi) * s
+            else:
+                tr, ti = xr * c + xi * s, xi * c - xr * s
+        low.append((er + tr, ei + ti))
+        high.append((er - tr, ei - ti))
+    return low + high
+
+
+def cos_sin(steps):
+    quarter = (steps + 64) >> 7
+    x = (steps - (quarter << 7)).astype(jnp.float32) * (2.0 * math.pi / 512)
+    y = x * x
+    s = x * (1.0 + y * (-1 / 6 + y * (1 / 120 + y * (-1 / 5040 + y * (1 / 362880)))))
+    c = 1.0 + y * (-0.5 + y * (1 / 24 + y * (-1 / 720 + y * (1 / 40320))))
+    odd = (quarter & 1) == 1
+    cosine = jnp.where(odd, s, c)
+    sine = jnp.where(odd, c, s)
+    cosine = jnp.where(((quarter + 1) & 2) == 2, -cosine, cosine)
+    sine = jnp.where((quarter & 2) == 2, -sine, sine)
+    return cosine, sine
+
+
+def calibrate_kernel(volt_ref, gain_ref, spread_ref, out_ref):
+    half = volt_ref.shape[1] // 2
+    halves = []
+    for p in range(2):
+        real = volt_ref[p, :half, :].astype(jnp.float32)
+        imag = volt_ref[p, half:, :].astype(jnp.float32)
+        gr = gain_ref[p, :half, :]
+        gi = gain_ref[p, half:, :]
+        both = jnp.concatenate(
+            [
+                (gr * real - gi * imag).astype(jnp.bfloat16),
+                (gr * imag + gi * real).astype(jnp.bfloat16),
+            ],
+            axis=0,
+        )
+        turned = lax.dot_general(
+            spread_ref[...], both, (((1,), (1,)), ((), ())), preferred_element_type=jnp.float32
+        )
+        halves.append(turned.reshape(TOUT * UP, 1, 8, 2 * half))
+    rows = jnp.concatenate(halves, axis=1).astype(jnp.bfloat16)
+    out_ref[0] = rows.reshape(TOUT, UP * 16, 2 * half)
+
+
+def beam_kernel(
+    n, x_ref, ns_ref, ew_ref, nb_ref, out_ref,
+    recv, wre, wim, sums, psc, pbuf, precv, turn,
+    send_sem, recv_sem, own_sem, psend_sem, precv_sem, pown_sem,
+):
+    me = lax.axis_index("chan")
+    barrier = pltpu.get_barrier_semaphore()
+
+    def greet(s, carry):
+        pl.semaphore_signal(
+            barrier, inc=1, device_id={"chan": lax.rem(me + s, n)}, device_id_type=MESH
+        )
+        return carry
+
+    lax.fori_loop(1, n, greet, 0)
+    pl.semaphore_wait(barrier, n - 1)
+
+    mine = pl.ds(pl.multiple_of(me * 128, 128), 128)
+
+    def volt_copy(u, s):
+        d = lax.rem(me + s, n)
+        return pltpu.make_async_remote_copy(
+            src_ref=x_ref.at[d, u],
+            dst_ref=recv.at[u, :, mine],
+            send_sem=send_sem.at[u, s],
+            recv_sem=recv_sem.at[u, s],
+            device_id={"chan": d},
+            device_id_type=MESH,
+        )
+
+    def own_copy(u):
+        return pltpu.make_async_copy(x_ref.at[me, u], recv.at[u, :, mine], own_sem.at[u])
+
+    def power_copy(u, s):
+        d = lax.rem(me + s, n)
+        return pltpu.make_async_remote_copy(
+            src_ref=pbuf.at[u, d],
+            dst_ref=precv.at[u, me],
+            send_sem=psend_sem.at[u, s],
+            recv_sem=precv_sem.at[u, s],
+            device_id={"chan": d},
+            device_id_type=MESH,
+        )
+
+    def own_power(u):
+        return pltpu.make_async_copy(pbuf.at[u, me], precv.at[u, me], pown_sem.at[u])
+
+    def each(make, act, u):
+        def one(s, carry):
+            getattr(make(u, s), act)()
+            return carry
+
+        lax.fori_loop(1, n, one, 0)
+
+    for u in range(TOUT):
+        each(volt_copy, "start", u)
+    for u in range(TOUT):
+        own_copy(u).start()
+
+    def table(s, carry):
+        feeds = pl.ds(pl.multiple_of(s * 64, 64), 64)
+        top = pl.ds(pl.multiple_of(s * 128, 128), 64)
+        low = pl.ds(pl.multiple_of(s * 128 + 64, 64), 64)
+        slope = ns_ref[feeds, :] * nb_ref[...]
+        for e in range(EWB):
+            cosine, sine = cos_sin((slope + ew_ref[feeds, e : e + 1]) & 511)
+            cols = slice(e * NSB, (e + 1) * NSB)
+            cosine = cosine.astype(jnp.bfloat16)
+            wre[top, cols] = cosine
+            wim[low, cols] = cosine
+            wim[top, cols] = sine.astype(jnp.bfloat16)
+            wre[low, cols] = (-sine).astype(jnp.bfloat16)
+        return carry
+
+    lax.fori_loop(0, n, table, 0)
+    left = lax.broadcasted_iota(jnp.int32, (16, 128), 1) < 64
+
+    for u in range(TOUT):
+        each(volt_copy, "wait_recv", u)
+        own_copy(u).wait()
+
+        def block(nb, carry, u=u):
+            cols = pl.ds(pl.multiple_of(nb * 256, 256), 256)
+            sums[0] = jnp.dot(recv[u], wre[:, cols], preferred_element_type=jnp.float32)
+            sums[1] = jnp.dot(recv[u], wim[:, cols], preferred_element_type=jnp.float32)
+            for lane in range(2):
+                at = slice(lane * 128, (lane + 1) * 128)
+                total = None
+                for p in range(2):
+                    bins = fft(
+                        [
+                            (
+                                sums[0, j * 16 + p * 8 : j * 16 + p * 8 + 8, at],
+                                sums[1, j * 16 + p * 8 : j * 16 + p * 8 + 8, at],
+                            )
+                            for j in range(UP)
+                        ]
+                    )
+                    power = [r * r + i * i for r, i in bins]
+                    total = power if p == 0 else [a + b for a, b in zip(total, power)]
+                for k in range(UP):
+                    part = total[k]
+                    part = part + pltpu.roll(part, 6, 0)
+                    part = part + pltpu.roll(part, 7, 0)
+                    psc[k : k + 1, :] = part[0:1]
+                    psc[UP + k : UP + k + 1, :] = part[4:5]
+                c0 = psc[:UP, :]
+                c1 = psc[UP:, :]
+                pair = (nb * 2 + lane) * 2
+                pbuf[u, pair] = jnp.where(left, c0, pltpu.roll(c1, 64, 1)).astype(jnp.bfloat16)
+                pbuf[u, pair + 1] = jnp.where(left, pltpu.roll(c0, 64, 1), c1).astype(jnp.bfloat16)
+            return carry
+
+        lax.fori_loop(0, BEAMS // 256, block, 0)
+        each(power_copy, "start", u)
+        own_power(u).start()
+
+    for u in range(TOUT):
+        each(volt_copy, "wait_send", u)
+
+    for u in range(TOUT):
+        each(power_copy, "wait_recv", u)
+        own_power(u).wait()
+
+        def gather(src, carry, u=u):
+            rows = precv[u, src].astype(jnp.float32)
+            first = pl.multiple_of(src * 32, 32)
+            turn[pl.ds(first, 16), :] = rows
+            turn[pl.ds(first + 16, 16), :] = pltpu.roll(rows, 64, 1)
+            return carry
+
+        lax.fori_loop(0, n, gather, 0)
+        beams = jnp.concatenate(
+            [turn[i * 128 : (i + 1) * 128, :].T[:64] for i in range(n * 32 // 128)], axis=1
+        )
+        baseline = jnp.sum(beams, axis=1, keepdims=True) / (n * 32)
+        out_ref[u] = beams / (baseline + eps_power)
+    for u in range(TOUT):
+        each(power_copy, "wait_send", u)
+
+
+def fused(n, voltages, gains, feed_cyl, feed_ns, ew_index, ns_beam):
+    half = voltages.shape[1]
+    samples = UP * DS * TOUT
+    flat = voltages.transpose(2, 0, 1, 3, 4).reshape(2, 2 * half, -1)
+    gain = gains.transpose(1, 0, 2).reshape(2, 2 * half, 1)
+    row = np.arange(2 * samples)
+    u, j, c, d = row // 128, row // 8 % UP, row // 4 % 2, row % DS
+    take = c * samples + (u * DS + d) * UP + j
+    spread = (jnp.asarray(take, jnp.int32)[:, None] == jnp.arange(2 * samples, dtype=jnp.int32)[None, :]).astype(
+        jnp.bfloat16
+    )
+    x = pl.pallas_call(
+        calibrate_kernel,
+        grid=(n,),
+        out_shape=jax.ShapeDtypeStruct((n, TOUT, 256, 128), jnp.bfloat16),
+        in_specs=[
+            pl.BlockSpec((2, 2 * half, 2 * samples), lambda i: (0, 0, i)),
+            pl.BlockSpec((2, 2 * half, 1), lambda i: (0, 0, 0)),
+            pl.BlockSpec((2 * samples, 2 * samples), lambda i: (0, 0)),
+        ],
+        out_specs=pl.BlockSpec((1, TOUT, 256, 128), lambda i: (i, 0, 0, 0)),
+    )(flat, gain, spread)
+    onehot = (feed_cyl[:, None] == jnp.arange(CYL, dtype=jnp.int32)[None, :]).astype(jnp.int32)
+    ew = jnp.sum(onehot[:, None, :] * ew_index[None, :, :], axis=2) * 8
+    vmem = pl.BlockSpec(memory_space=pltpu.VMEM)
+    dma = pltpu.SemaphoreType.DMA
+    out = pl.pallas_call(
+        functools.partial(beam_kernel, n),
+        out_shape=jax.ShapeDtypeStruct((TOUT, BEAMS // n, n * 32), jnp.float32),
+        in_specs=[pl.BlockSpec(memory_space=pl.ANY), vmem, vmem, vmem],
+        out_specs=vmem,
+        scratch_shapes=[
+            pltpu.VMEM((TOUT, 256, n * 128), jnp.bfloat16),
+            pltpu.VMEM((2 * FEEDS, BEAMS), jnp.bfloat16),
+            pltpu.VMEM((2 * FEEDS, BEAMS), jnp.bfloat16),
+            pltpu.VMEM((2, 256, 256), jnp.float32),
+            pltpu.VMEM((2 * UP, 128), jnp.float32),
+            pltpu.VMEM((TOUT, n, 16, 128), jnp.bfloat16),
+            pltpu.VMEM((TOUT, n, 16, 128), jnp.bfloat16),
+            pltpu.VMEM((n * 32, 128), jnp.float32),
+            dma((TOUT, n)), dma((TOUT, n)), dma((TOUT,)),
+            dma((TOUT, n)), dma((TOUT, n)), dma((TOUT,)),
+        ],
+        compiler_params=pltpu.CompilerParams(
+            collective_id=0, has_side_effects=True, vmem_limit_bytes=48 << 20
+        ),
+    )(x, feed_ns[:, None], ew, ns_beam[None, :])
+    return out.transpose(1, 0, 2)
+
 
 def solution(mesh):
     placed = (P(None, "chan", None, None, "grp"), P(None, None, "chan"), P(), P(), P(), P())
+    n = mesh.shape["chan"]
+
+    def part(voltages, gains, feed_cyl, feed_ns, ew_index, ns_beam):
+        fits = voltages.shape == (2, 64, 2, 2 * n, UP * DS * TOUT) and n * 64 == FEEDS
+        run = functools.partial(fused, n) if fits else shards
+        return run(voltages, gains, feed_cyl, feed_ns, ew_index, ns_beam)
+
     return jax.shard_map(
-        shards, mesh=mesh, in_specs=placed, out_specs=P("chan", "grp", None), check_vma=False
-    )
+        part, mesh=mesh, in_specs=placed, out_specs=P("chan", "grp", None), check_vma=False
+    )

time: 247 us -> 148 us (0.60)
  Pallas kernels: 0 us -> 128 us
  blocking collectives: 85 us -> 0 us
  other arithmetic: 82.6 us -> 1.11 us
  local copies, waits for them, and re-layouts: 50.2 us -> 18.3 us
  matrix products: 20.8 us -> 0 us
  starting transfers between devices: 7.58 us -> 0 us
    pallas_call x0 -> x2, Pallas kernels: none -> 128 us  [the longest x1 113 us: fused(): pl.pallas_call(functools.partial(beam_kernel, n), out_shape=jax.ShapeDtyp...]
    psum x1 -> x0, blocking collectives: 67.9 us -> none  [shards(): band_sum = lax.psum(jnp.sum(beam_power, axis=(2, 3)), 'chan')]
    concatenate x1 -> x0, other arithmetic: 36.8 us -> none  [phase_table(): return jnp.concatenate([upper_rows, lower_rows], axis=0)]
    dot_general x2 -> x0, matrix products: 20.8 us -> none  [the longest x1 12.6 us: shards(): jnp.einsum('rfpct,rfq->pctq', arrived, weights, preferred_element_type=jn...]
    convert_element_type x4 -> x2, other arithmetic: 21.5 us -> 0.95 us  [the longest x1 0.95 us: fused(): (jnp.asarray(take, jnp.int32)[:, None] == jnp.arange(2 * samples, dtype=j...]
    dot_general x2 -> x0, local copies, waits for them, and re-layouts: 18.1 us -> none  [shards(): jnp.einsum('rfpct,rfq->pctq', arrived, weights, preferred_element_type=jn...]
    all_to_all x1 -> x0, blocking collectives: 17.1 us -> none  [shards(): lax.all_to_all(normed, 'chan', split_axis=0, concat_axis=2, tiled=True)]
    neg x2 -> x0, other arithmetic: 15.8 us -> none  [the longest x1 15.8 us: phase_table(): lower_rows = jnp.concatenate([-sine_part, cosine], axis=1)]
  transfers between devices with their start and end apart: 1 -> 0, of which waited for: 0 -> 0; matrix products, arithmetic and copies ran while one was open for 35% -> 0% of each run, Pallas kernels for 0% -> 0%
where the time goes in v1:
time: 148 us; the launch traced here: 147 us
  Pallas kernels  128 us (86%)
  local copies, waits for them, and re-layouts  18.3 us (12%)
    pallas_call x1, Pallas kernels, fused(): pl.pallas_call(functools.partial(beam_kernel, n), out_shape=jax.ShapeDtyp...  113 us
    pallas_call x1, Pallas kernels, fused(): pl.pallas_call(calibrate_kernel, grid=(n,), out_shape=jax.ShapeDtypeStruc...  14.4 us
    reshape x2, local copies, waits for them, and re-layouts, fused(): flat = voltages.transpose(2, 0, 1, 3, 4).reshape(2, 2 * half, -1)  13.8 us

profile of v1, /device:TPU:0, one launch (start us, length us, event | category | flops | bytes accessed | tf_op | source)
XLA Modules:
  0.0 147.0 jit_solution(742313602263170827)
XLA Ops:
  0.0 6.9 %reshape.28 = bf16[2,128,8192]{2,0,1:T(2,128)(2,1)} reshape(bf16[2,2,64,32,256]{4,3,0,2,1:T(8,128)(2,1)} %bitcast.11) | data formatting | bytes 8388608 | tf_op jit(solution)/shard_map/reshape | solution.py:289
  6.9 0.0 copy-start.4
  6.9 0.0 copy-start.6
  6.9 6.8 %copy.29.volt_ref = bf16[2,128,8192]{2,1,0:T(8,128)(2,1)} copy(bf16[2,128,8192]{2,0,1:T(2,128)(2,1)} %reshape.28) | data formatting | bytes 8388608 | tf_op jit(solution)/shard_map/reshape | solution.py:289
  13.8 0.0 copy-done.4
  13.8 0.9 fusion.spread_ref
  14.7 0.0 copy-done.6
  14.7 0.8 reshape.29.gain_ref
  15.5 0.0 copy-start.3
  15.5 0.0 copy-start.5
  15.5 0.0 copy-start.2
  15.5 0.0 copy-start.1
  15.5 14.4 %shard_map.73.x_ref = bf16[16,4,256,128]{3,2,1,0:T(8,128)(2,1)} custom-call(bf16[2,128,8192]{2,1,0:T(8,128)(2,1)} %copy.29.volt_ref, f32[2,128,1]{2,1,0:T(8,128)} %reshape.29.gain_ref, bf16[512,512]{1,0:T(8,128)(2,1)} %fusion.spread_ref), custom_call_target="tpu_custom_call" | custom-call | tf_op jit(solution)/shard_map/pallas_call | solution.py:297
  30.0 0.0 copy-done.3
  30.0 0.0 copy-done.5
  30.0 0.1 multiply_reduce_fusion
  30.1 0.2 copy.25
  30.4 0.0 copy-done.2
  30.4 0.2 copy.27.ns_ref
  30.6 0.0 copy-done.1
  30.6 0.0 copy-start
  30.6 2.2 %copy-done = bf16[16,4,256,128]{3,2,1,0:T(8,128)(2,1)S(1)} copy-done((bf16[16,4,256,128]{3,2,1,0:T(8,128)(2,1)S(1)}, bf16[16,4,256,128]{3,2,1,0:T(8,128)(2,1)}, u32[]{:S(2)}) %copy-start) | copy-done | bytes 4194328
  32.8 113.1 %shard_map.74 = f32[4,64,512]{2,1,0:T(8,128)S(1)} custom-call(bf16[16,4,256,128]{3,2,1,0:T(8,128)(2,1)S(1)} %copy-done, s32[1024,1]{1,0:T(8,128)S(1)} %copy.27.ns_ref, s32[1024,4]{1,0:T(8,128)S(1)} %broadcast_multiply_fusion.ew_ref, s32[1,256]{1,0:T(1,128)S(1)} %bitcast.10), custom_call_target="tpu_custom_call" | custom-call | tf_op jit(solution)/shard_map/pallas_call | solution.py:312
  145.9 1.1 copy.28
  (3 shorter events, 0.0 us)
Async XLA Ops:
  6.9 6.8 %copy-start.4 = (s32[512]{0:T(512)S(1)}, s32[512]{0:T(512)}, u32[]{:S(2)}) copy-start(s32[512]{0:T(512)} %constant.6.clone) | copy-start | bytes 6148
  6.9 7.8 %copy-start.6 = (f32[2,2,64]{2,1,0:T(2,128)S(1)}, f32[2,2,64]{2,1,0:T(2,128)}, u32[]{:S(2)}) copy-start(f32[2,2,64]{2,1,0:T(2,128)} %param.8) | copy-start | bytes 3076
  15.5 14.5 %copy-start.3 = (s32[1024]{0:T(1024)S(1)}, s32[1024]{0:T(1024)}, u32[]{:S(2)}) copy-start(s32[1024]{0:T(1024)} %param.9) | copy-start | bytes 12292
  15.5 14.5 %copy-start.5 = (s32[4,4]{1,0:T(4,128)S(1)}, s32[4,4]{1,0:T(4,128)}, u32[]{:S(2)}) copy-start(s32[4,4]{1,0:T(4,128)} %param.11) | copy-start | bytes 196
  15.5 14.9 %copy-start.2 = (s32[1024]{0:T(1024)S(1)}, s32[1024]{0:T(1024)}, u32[]{:S(2)}) copy-start(s32[1024]{0:T(1024)} %param.10) | copy-start | bytes 12292
  15.5 15.1 %copy-start.1 = (s32[256]{0:T(256)S(1)}, s32[256]{0:T(256)}, u32[]{:S(2)}) copy-start(s32[256]{0:T(256)} %param.12) | copy-start | bytes 3076
  30.6 2.2 %copy-start = (bf16[16,4,256,128]{3,2,1,0:T(8,128)(2,1)S(1)}, bf16[16,4,256,128]{3,2,1,0:T(8,128)(2,1)}, u32[]{:S(2)}) copy-start(bf16[16,4,256,128]{3,2,1,0:T(8,128)(2,1)} %shard_map.73.x_ref) | copy-start | bytes 12582916

commit v2 on v1

--- a/solution.py
+++ b/solution.py
@@ -3,7 +3,6 @@
 
 import jax
 import jax.numpy as jnp
-import numpy as np
 from jax import lax
 from jax.experimental import pallas as pl
 from jax.experimental.pallas import tpu as pltpu
@@ -119,35 +118,15 @@
     return cosine, sine
 
 
-def calibrate_kernel(volt_ref, gain_ref, spread_ref, out_ref):
-    half = volt_ref.shape[1] // 2
-    halves = []
-    for p in range(2):
-        real = volt_ref[p, :half, :].astype(jnp.float32)
-        imag = volt_ref[p, half:, :].astype(jnp.float32)
-        gr = gain_ref[p, :half, :]
-        gi = gain_ref[p, half:, :]
-        both = jnp.concatenate(
-            [
-                (gr * real - gi * imag).astype(jnp.bfloat16),
-                (gr * imag + gi * real).astype(jnp.bfloat16),
-            ],
-            axis=0,
-        )
-        turned = lax.dot_general(
-            spread_ref[...], both, (((1,), (1,)), ((), ())), preferred_element_type=jnp.float32
-        )
-        halves.append(turned.reshape(TOUT * UP, 1, 8, 2 * half))
-    rows = jnp.concatenate(halves, axis=1).astype(jnp.bfloat16)
-    out_ref[0] = rows.reshape(TOUT, UP * 16, 2 * half)
-
-
 def beam_kernel(
-    n, x_ref, ns_ref, ew_ref, nb_ref, out_ref,
+    n, volt_ref, gain_ref, cyl_ref, ns_ref, ew_ref, nb_ref, out_ref,
+    volt, wide, spread, gcol, ccol, ncol, xin, x_ref,
     recv, wre, wim, sums, psc, pbuf, precv, turn,
-    send_sem, recv_sem, own_sem, psend_sem, precv_sem, pown_sem,
+    volt_sem, send_sem, recv_sem, own_sem, psend_sem, precv_sem, pown_sem,
 ):
     me = lax.axis_index("chan")
+    fetch = pltpu.make_async_copy(volt_ref, volt, volt_sem)
+    fetch.start()
     barrier = pltpu.get_barrier_semaphore()
 
     def greet(s, carry):
@@ -157,6 +136,32 @@
         return carry
 
     lax.fori_loop(1, n, greet, 0)
+
+    row = lax.broadcasted_iota(jnp.int32, spread.shape, 0)
+    take = ((row >> 2) & 1) * 256 + ((row >> 7) * DS + (row & 3)) * UP + ((row >> 3) & 15)
+    lane = lax.broadcasted_iota(jnp.int32, spread.shape, 1)
+    spread[...] = jnp.where(take == lane, 1.0, 0.0).astype(jnp.bfloat16)
+    for r in range(2):
+        for p in range(2):
+            gcol[r, p] = jnp.broadcast_to(gain_ref[r, p : p + 1, :], (128, 64)).T
+    for i in range(FEEDS // 128):
+        rows = slice(i * 128, (i + 1) * 128)
+        ccol[rows, :] = jnp.broadcast_to(cyl_ref[i : i + 1, :], (128, 128)).T
+        ncol[rows, :] = jnp.broadcast_to(ns_ref[i : i + 1, :], (128, 128)).T
+
+    fetch.wait()
+
+    def widen(i, carry):
+        first = pl.multiple_of(i * 8 * 2 * n, 8 * 2 * n)
+        for r in range(2):
+            for p in range(2):
+                part = volt[r, pl.ds(pl.multiple_of(i * 8, 8), 8), p].astype(jnp.float32)
+                part = part.reshape(8 * 2 * n, 256)
+                for h in range(2):
+                    wide[r, p, h, pl.ds(first, 8 * 2 * n), :] = part[:, h * 128 : (h + 1) * 128]
+        return carry
+
+    lax.fori_loop(0, 8, widen, 0)
     pl.semaphore_wait(barrier, n - 1)
 
     mine = pl.ds(pl.multiple_of(me * 128, 128), 128)
@@ -196,7 +201,37 @@
 
         lax.fori_loop(1, n, one, 0)
 
-    for u in range(TOUT):
+    def produce(i, carry):
+        s = lax.rem(i + n // 2, n)
+        d = lax.rem(me + s, n)
+        for p in range(2):
+            for c in range(2):
+                for h in range(2):
+                    at = pl.ds(d * 2 + c, 64, stride=2 * n)
+                    real = wide[0, p, h, at, :]
+                    imag = wide[1, p, h, at, :]
+                    gr = gcol[0, p]
+                    gi = gcol[1, p]
+                    cols = slice(c * 256 + h * 128, c * 256 + h * 128 + 128)
+                    xin[p * 128 : p * 128 + 64, cols] = (gr * real - gi * imag).astype(jnp.bfloat16)
+                    xin[p * 128 + 64 : p * 128 + 128, cols] = (gr * imag + gi * real).astype(jnp.bfloat16)
+        turned = lax.dot_general(
+            spread[...], xin[...], (((1,), (1,)), ((), ())), preferred_element_type=jnp.float32
+        )
+        rows = jnp.concatenate(
+            [turned[:, :128].reshape(TOUT * UP, 1, 8, 128), turned[:, 128:].reshape(TOUT * UP, 1, 8, 128)],
+            axis=1,
+        )
+        x_ref[d] = rows.astype(jnp.bfloat16).reshape(TOUT, UP * 16, 128)
+
+        @pl.when(s > 0)
+        def _():
+            volt_copy(0, s).start()
+
+        return carry
+
+    lax.fori_loop(0, n, produce, 0)
+    for u in range(1, TOUT):
         each(volt_copy, "start", u)
     for u in range(TOUT):
         own_copy(u).start()
@@ -205,15 +240,22 @@
         feeds = pl.ds(pl.multiple_of(s * 64, 64), 64)
         top = pl.ds(pl.multiple_of(s * 128, 128), 64)
         low = pl.ds(pl.multiple_of(s * 128 + 64, 64), 64)
-        slope = ns_ref[feeds, :] * nb_ref[...]
-        for e in range(EWB):
-            cosine, sine = cos_sin((slope + ew_ref[feeds, e : e + 1]) & 511)
-            cols = slice(e * NSB, (e + 1) * NSB)
-            cosine = cosine.astype(jnp.bfloat16)
-            wre[top, cols] = cosine
-            wim[low, cols] = cosine
-            wim[top, cols] = sine.astype(jnp.bfloat16)
-            wre[low, cols] = (-sine).astype(jnp.bfloat16)
+        cyl = ccol[feeds, :]
+        for h in range(2):
+            slope = ncol[feeds, :] * nb_ref[h : h + 1, :]
+            for e in range(EWB):
+                shift = jnp.where(
+                    cyl < 2,
+                    jnp.where(cyl == 0, ew_ref[e, 0], ew_ref[e, 1]),
+                    jnp.where(cyl == 2, ew_ref[e, 2], ew_ref[e, 3]),
+                )
+                cosine, sine = cos_sin((slope + shift * 8) & 511)
+                cols = slice(e * NSB + h * 128, e * NSB + h * 128 + 128)
+                cosine = cosine.astype(jnp.bfloat16)
+                wre[top, cols] = cosine
+                wim[low, cols] = cosine
+                wim[top, cols] = sine.astype(jnp.bfloat16)
+                wre[low, cols] = (-sine).astype(jnp.bfloat16)
         return carry
 
     lax.fori_loop(0, n, table, 0)
@@ -251,8 +293,8 @@
                 c0 = psc[:UP, :]
                 c1 = psc[UP:, :]
                 pair = (nb * 2 + lane) * 2
-                pbuf[u, pair] = jnp.where(left, c0, pltpu.roll(c1, 64, 1)).astype(jnp.bfloat16)
-                pbuf[u, pair + 1] = jnp.where(left, pltpu.roll(c0, 64, 1), c1).astype(jnp.bfloat16)
+                pbuf[u, pair] = jnp.where(left, c0, pltpu.roll(c1, 64, 1))
+                pbuf[u, pair + 1] = jnp.where(left, pltpu.roll(c0, 64, 1), c1)
             return carry
 
         lax.fori_loop(0, BEAMS // 256, block, 0)
@@ -267,7 +309,7 @@
         own_power(u).wait()
 
         def gather(src, carry, u=u):
-            rows = precv[u, src].astype(jnp.float32)
+            rows = precv[u, src]
             first = pl.multiple_of(src * 32, 32)
             turn[pl.ds(first, 16), :] = rows
             turn[pl.ds(first + 16, 16), :] = pltpu.roll(rows, 64, 1)
@@ -284,52 +326,43 @@
 
 
 def fused(n, voltages, gains, feed_cyl, feed_ns, ew_index, ns_beam):
-    half = voltages.shape[1]
-    samples = UP * DS * TOUT
-    flat = voltages.transpose(2, 0, 1, 3, 4).reshape(2, 2 * half, -1)
-    gain = gains.transpose(1, 0, 2).reshape(2, 2 * half, 1)
-    row = np.arange(2 * samples)
-    u, j, c, d = row // 128, row // 8 % UP, row // 4 % 2, row % DS
-    take = c * samples + (u * DS + d) * UP + j
-    spread = (jnp.asarray(take, jnp.int32)[:, None] == jnp.arange(2 * samples, dtype=jnp.int32)[None, :]).astype(
-        jnp.bfloat16
-    )
-    x = pl.pallas_call(
-        calibrate_kernel,
-        grid=(n,),
-        out_shape=jax.ShapeDtypeStruct((n, TOUT, 256, 128), jnp.bfloat16),
-        in_specs=[
-            pl.BlockSpec((2, 2 * half, 2 * samples), lambda i: (0, 0, i)),
-            pl.BlockSpec((2, 2 * half, 1), lambda i: (0, 0, 0)),
-            pl.BlockSpec((2 * samples, 2 * samples), lambda i: (0, 0)),
-        ],
-        out_specs=pl.BlockSpec((1, TOUT, 256, 128), lambda i: (i, 0, 0, 0)),
-    )(flat, gain, spread)
-    onehot = (feed_cyl[:, None] == jnp.arange(CYL, dtype=jnp.int32)[None, :]).astype(jnp.int32)
-    ew = jnp.sum(onehot[:, None, :] * ew_index[None, :, :], axis=2) * 8
     vmem = pl.BlockSpec(memory_space=pltpu.VMEM)
     dma = pltpu.SemaphoreType.DMA
     out = pl.pallas_call(
         functools.partial(beam_kernel, n),
         out_shape=jax.ShapeDtypeStruct((TOUT, BEAMS // n, n * 32), jnp.float32),
-        in_specs=[pl.BlockSpec(memory_space=pl.ANY), vmem, vmem, vmem],
+        in_specs=[
+            pl.BlockSpec(memory_space=pl.ANY), vmem, vmem, vmem,
+            pl.BlockSpec(memory_space=pltpu.SMEM), vmem,
+        ],
         out_specs=vmem,
         scratch_shapes=[
+            pltpu.VMEM(voltages.shape, jnp.bfloat16),
+            pltpu.VMEM((2, 2, 2, 64 * 2 * n, 128), jnp.float32),
+            pltpu.VMEM((512, 512), jnp.bfloat16),
+            pltpu.VMEM((2, 2, 64, 128), jnp.float32),
+            pltpu.VMEM((FEEDS, 128), jnp.int32),
+            pltpu.VMEM((FEEDS, 128), jnp.int32),
+            pltpu.VMEM((256, 512), jnp.bfloat16),
+            pltpu.VMEM((n, TOUT, 256, 128), jnp.bfloat16),
             pltpu.VMEM((TOUT, 256, n * 128), jnp.bfloat16),
             pltpu.VMEM((2 * FEEDS, BEAMS), jnp.bfloat16),
             pltpu.VMEM((2 * FEEDS, BEAMS), jnp.bfloat16),
             pltpu.VMEM((2, 256, 256), jnp.float32),
             pltpu.VMEM((2 * UP, 128), jnp.float32),
-            pltpu.VMEM((TOUT, n, 16, 128), jnp.bfloat16),
-            pltpu.VMEM((TOUT, n, 16, 128), jnp.bfloat16),
+            pltpu.VMEM((TOUT, n, 16, 128), jnp.float32),
+            pltpu.VMEM((TOUT, n, 16, 128), jnp.float32),
             pltpu.VMEM((n * 32, 128), jnp.float32),
-            dma((TOUT, n)), dma((TOUT, n)), dma((TOUT,)),
+            dma, dma((TOUT, n)), dma((TOUT, n)), dma((TOUT,)),
             dma((TOUT, n)), dma((TOUT, n)), dma((TOUT,)),
         ],
         compiler_params=pltpu.CompilerParams(
-            collective_id=0, has_side_effects=True, vmem_limit_bytes=48 << 20
+            collective_id=0, has_side_effects=True, vmem_limit_bytes=56 << 20
         ),
-    )(x, feed_ns[:, None], ew, ns_beam[None, :])
+    )(
+        voltages, gains, feed_cyl.reshape(-1, 128), feed_ns.reshape(-1, 128),
+        ew_index, ns_beam.reshape(-1, 128),
+    )
     return out.transpose(1, 0, 2)
 
 

time: 148 us -> 121 us (0.82)
  local copies, waits for them, and re-layouts: 18.3 us -> 2.17 us
  Pallas kernels: 128 us -> 119 us
    reshape x3 -> x0, local copies, waits for them, and re-layouts: 14.5 us -> none  [the longest x2 13.8 us: fused(): flat = voltages.transpose(2, 0, 1, 3, 4).reshape(2, 2 * half, -1)]
    pallas_call x1 -> x0, Pallas kernels: 14.4 us -> none  [fused(): pl.pallas_call(calibrate_kernel, grid=(n,), out_shape=jax.ShapeDtypeStruc...]
    pallas_call x1, Pallas kernels: 113 us -> 119 us  [fused(): pl.pallas_call(functools.partial(beam_kernel, n), out_shape=jax.ShapeDtyp...]
    unnamed x14 -> x0, local copies, waits for them, and re-layouts: 2.2 us -> none
where the time goes in v2:
time: 121 us
  Pallas kernels  119 us (98%)
  local copies, waits for them, and re-layouts  2.17 us (2%)
    pallas_call x1, Pallas kernels, fused(): pl.pallas_call(functools.partial(beam_kernel, n), out_shape=jax.ShapeDtyp...  119 us

profile of v2, /device:TPU:0, one launch (start us, length us, event | category | flops | bytes accessed | tf_op | source)
XLA Modules:
  0.0 120.7 jit_solution(12778755319131520849)
XLA Ops:
  0.0 118.6 %shard_map.64 = f32[4,64,512]{2,1,0:T(8,128)} custom-call(bf16[2,64,2,32,256]{4,3,2,1,0:T(8,128)(2,1)} %volt_ref.1, f32[2,2,64]{2,1,0:T(2,128)} %gain_ref.1, s32[8,128]{1,0:T(8,128)} %bitcast.5, s32[8,128]{1,0:T(8,128)} %bitcast.6, s32[4,4]{1,0:T(4,128)} %ew_ref.1, s32[2,128]{1,0:T(2,128)} %bitcast.7), custom_call_target="tpu_custom_call" | custom-call | tf_op jit(solution)/shard_map/pallas_call | solution.py:331
  118.6 2.2 %copy.7 = f32[64,4,512]{2,1,0:T(4,128)} copy(f32[64,4,512]{2,0,1:T(8,128)} %bitcast.4) | data formatting | bytes 1048576 | tf_op jit(solution)/shard_map/transpose | solution.py:366

commit v3 on v2

--- a/solution.py
+++ b/solution.py
@@ -125,8 +125,16 @@
     volt_sem, send_sem, recv_sem, own_sem, psend_sem, precv_sem, pown_sem,
 ):
     me = lax.axis_index("chan")
-    fetch = pltpu.make_async_copy(volt_ref, volt, volt_sem)
-    fetch.start()
+
+    def fetch(i):
+        feeds = pl.ds(pl.multiple_of(i * 8, 8), 8)
+        return pltpu.make_async_copy(volt_ref.at[:, feeds], volt.at[:, feeds], volt_sem.at[i])
+
+    def begin(i, carry):
+        fetch(i).start()
+        return carry
+
+    lax.fori_loop(0, 8, begin, 0)
     barrier = pltpu.get_barrier_semaphore()
 
     def greet(s, carry):
@@ -144,14 +152,8 @@
     for r in range(2):
         for p in range(2):
             gcol[r, p] = jnp.broadcast_to(gain_ref[r, p : p + 1, :], (128, 64)).T
-    for i in range(FEEDS // 128):
-        rows = slice(i * 128, (i + 1) * 128)
-        ccol[rows, :] = jnp.broadcast_to(cyl_ref[i : i + 1, :], (128, 128)).T
-        ncol[rows, :] = jnp.broadcast_to(ns_ref[i : i + 1, :], (128, 128)).T
-
-    fetch.wait()
-
     def widen(i, carry):
+        fetch(i).wait()
         first = pl.multiple_of(i * 8 * 2 * n, 8 * 2 * n)
         for r in range(2):
             for p in range(2):
@@ -235,6 +237,11 @@
         each(volt_copy, "start", u)
     for u in range(TOUT):
         own_copy(u).start()
+
+    for i in range(FEEDS // 128):
+        rows = slice(i * 128, (i + 1) * 128)
+        ccol[rows, :] = jnp.broadcast_to(cyl_ref[i : i + 1, :], (128, 128)).T
+        ncol[rows, :] = jnp.broadcast_to(ns_ref[i : i + 1, :], (128, 128)).T
 
     def table(s, carry):
         feeds = pl.ds(pl.multiple_of(s * 64, 64), 64)
@@ -259,13 +266,15 @@
         return carry
 
     lax.fori_loop(0, n, table, 0)
+    blocks = BEAMS // 256
     left = lax.broadcasted_iota(jnp.int32, (16, 128), 1) < 64
 
     for u in range(TOUT):
         each(volt_copy, "wait_recv", u)
         own_copy(u).wait()
 
-        def block(nb, carry, u=u):
+        def block(i, carry, u=u):
+            nb = lax.rem(i + me * blocks // n + blocks // 2, blocks)
             cols = pl.ds(pl.multiple_of(nb * 256, 256), 256)
             sums[0] = jnp.dot(recv[u], wre[:, cols], preferred_element_type=jnp.float32)
             sums[1] = jnp.dot(recv[u], wim[:, cols], preferred_element_type=jnp.float32)
@@ -295,10 +304,16 @@
                 pair = (nb * 2 + lane) * 2
                 pbuf[u, pair] = jnp.where(left, c0, pltpu.roll(c1, 64, 1))
                 pbuf[u, pair + 1] = jnp.where(left, pltpu.roll(c0, 64, 1), c1)
+            for q in range(n // blocks):
+                s = lax.rem(nb * (n // blocks) + q - me + n, n)
+
+                @pl.when(s > 0)
+                def _(s=s):
+                    power_copy(u, s).start()
+
             return carry
 
-        lax.fori_loop(0, BEAMS // 256, block, 0)
-        each(power_copy, "start", u)
+        lax.fori_loop(0, blocks, block, 0)
         own_power(u).start()
 
     for u in range(TOUT):
@@ -332,7 +347,7 @@
         functools.partial(beam_kernel, n),
         out_shape=jax.ShapeDtypeStruct((TOUT, BEAMS // n, n * 32), jnp.float32),
         in_specs=[
-            pl.BlockSpec(memory_space=pl.ANY), vmem, vmem, vmem,
+            pl.BlockSpec(memory_space=pltpu.HBM), vmem, vmem, vmem,
             pl.BlockSpec(memory_space=pltpu.SMEM), vmem,
         ],
         out_specs=vmem,
@@ -353,11 +368,11 @@
             pltpu.VMEM((TOUT, n, 16, 128), jnp.float32),
             pltpu.VMEM((TOUT, n, 16, 128), jnp.float32),
             pltpu.VMEM((n * 32, 128), jnp.float32),
-            dma, dma((TOUT, n)), dma((TOUT, n)), dma((TOUT,)),
+            dma((8,)), dma((TOUT, n)), dma((TOUT, n)), dma((TOUT,)),
             dma((TOUT, n)), dma((TOUT, n)), dma((TOUT,)),
         ],
         compiler_params=pltpu.CompilerParams(
-            collective_id=0, has_side_effects=True, vmem_limit_bytes=56 << 20
+            collective_id=0, has_side_effects=True, vmem_limit_bytes=40 << 20
         ),
     )(
         voltages, gains, feed_cyl.reshape(-1, 128), feed_ns.reshape(-1, 128),

time: 121 us -> 125 us (1.033)
  local copies, waits for them, and re-layouts: 2.17 us -> 6.73 us
    unnamed x0 -> x12, local copies, waits for them, and re-layouts: none -> 5.6 us
where the time goes in v3:
time: 125 us; the launch traced here: 124 us
  Pallas kernels  118 us (94%)
  local copies, waits for them, and re-layouts  6.73 us (5%)
    pallas_call x1, Pallas kernels, fused(): pl.pallas_call(functools.partial(beam_kernel, n), out_shape=jax.ShapeDtyp...  118 us
    unnamed x12, local copies, waits for them, and re-layouts  5.6 us

profile of v3, /device:TPU:0, one launch (start us, length us, event | category | flops | bytes accessed | tf_op | source)
XLA Modules:
  0.0 124.3 jit_solution(3806287972322176814)
XLA Ops:
  0.0 0.0 copy-start
  0.0 2.2 %copy-done = bf16[2,64,2,32,256]{4,3,2,1,0:T(8,128)(2,1)S(1)} copy-done((bf16[2,64,2,32,256]{4,3,2,1,0:T(8,128)(2,1)S(1)}, bf16[2,64,2,32,256]{4,3,2,1,0:T(8,128)(2,1)}, u32[]{:S(2)}) %copy-start) | copy-done | bytes 4194328
  2.2 0.0 copy-start.1
  2.2 0.7 copy-done.1
  2.9 0.0 copy-start.2
  2.9 0.7 copy-done.2
  3.6 0.0 copy-start.3
  3.6 0.7 copy-done.3
  4.2 0.0 copy-start.4
  4.2 0.7 copy-done.4
  4.9 0.0 copy-start.5
  4.9 0.7 copy-done.5
  5.6 117.5 %shard_map.64 = f32[4,64,512]{2,1,0:T(8,128)S(1)} custom-call(bf16[2,64,2,32,256]{4,3,2,1,0:T(8,128)(2,1)S(1)} %copy-done, f32[2,2,64]{2,1,0:T(2,128)S(1)} %copy-done.3, s32[8,128]{1,0:T(8,128)S(1)} %bitcast.5, s32[8,128]{1,0:T(8,128)S(1)} %bitcast.6, s32[4,4]{1,0:T(4,128)S(1)} %copy-done.4, s32[2,128]{1,0:T(2,128)S(1)} %bitcast.7), custom_call_target="tpu_custom_call" | custom-call | tf_op jit(solution)/shard_map/pallas_call | solution.py:346
  123.1 1.1 copy.7
Async XLA Ops:
  0.0 2.2 %copy-start = (bf16[2,64,2,32,256]{4,3,2,1,0:T(8,128)(2,1)S(1)}, bf16[2,64,2,32,256]{4,3,2,1,0:T(8,128)(2,1)}, u32[]{:S(2)}) copy-start(bf16[2,64,2,32,256]{4,3,2,1,0:T(8,128)(2,1)} %volt_ref.1) | copy-start | bytes 12582916
  2.2 0.7 copy-start.1
  2.9 0.7 copy-start.2
  3.6 0.7 copy-start.3
  4.2 0.7 copy-start.4
  4.9 0.7 copy-start.5

commit v4 on v3

--- a/solution.py
+++ b/solution.py
@@ -347,7 +347,7 @@
         functools.partial(beam_kernel, n),
         out_shape=jax.ShapeDtypeStruct((TOUT, BEAMS // n, n * 32), jnp.float32),
         in_specs=[
-            pl.BlockSpec(memory_space=pltpu.HBM), vmem, vmem, vmem,
+            pl.BlockSpec(memory_space=pl.ANY), vmem, vmem, vmem,
             pl.BlockSpec(memory_space=pltpu.SMEM), vmem,
         ],
         out_specs=vmem,
@@ -372,7 +372,7 @@
             dma((TOUT, n)), dma((TOUT, n)), dma((TOUT,)),
         ],
         compiler_params=pltpu.CompilerParams(
-            collective_id=0, has_side_effects=True, vmem_limit_bytes=40 << 20
+            collective_id=0, has_side_effects=True, vmem_limit_bytes=56 << 20
         ),
     )(
         voltages, gains, feed_cyl.reshape(-1, 128), feed_ns.reshape(-1, 128),

time: 125 us -> 121 us (0.968)
  local copies, waits for them, and re-layouts: 6.73 us -> 2.17 us
    unnamed x12 -> x0, local copies, waits for them, and re-layouts: 5.6 us -> none
where the time goes in v4:
time: 121 us; the launch traced here: 120 us
  Pallas kernels  118 us (98%)
  local copies, waits for them, and re-layouts  2.17 us (2%)
    pallas_call x1, Pallas kernels, fused(): pl.pallas_call(functools.partial(beam_kernel, n), out_shape=jax.ShapeDtyp...  118 us

profile of v4, /device:TPU:0, one launch (start us, length us, event | category | flops | bytes accessed | tf_op | source)
XLA Modules:
  0.0 120.5 jit_solution(5329028240331020535)
XLA Ops:
  0.0 118.3 %shard_map.64 = f32[4,64,512]{2,1,0:T(8,128)} custom-call(bf16[2,64,2,32,256]{4,3,2,1,0:T(8,128)(2,1)} %volt_ref.1, f32[2,2,64]{2,1,0:T(2,128)} %gain_ref.1, s32[8,128]{1,0:T(8,128)} %bitcast.5, s32[8,128]{1,0:T(8,128)} %bitcast.6, s32[4,4]{1,0:T(4,128)} %ew_ref.1, s32[2,128]{1,0:T(2,128)} %bitcast.7), custom_call_target="tpu_custom_call" | custom-call | tf_op jit(solution)/shard_map/pallas_call | solution.py:346
  118.3 2.2 %copy.7 = f32[64,4,512]{2,1,0:T(4,128)} copy(f32[64,4,512]{2,0,1:T(8,128)} %bitcast.4) | data formatting | bytes 1048576 | tf_op jit(solution)/shard_map/transpose | solution.py:381

commit v5 on v4

--- a/solution.py
+++ b/solution.py
@@ -269,7 +269,27 @@
     blocks = BEAMS // 256
     left = lax.broadcasted_iota(jnp.int32, (16, 128), 1) < 64
 
+    def finish(u):
+        each(power_copy, "wait_recv", u)
+        own_power(u).wait()
+
+        def gather(src, carry):
+            rows = precv[u, src]
+            first = pl.multiple_of(src * 32, 32)
+            turn[pl.ds(first, 16), :] = rows
+            turn[pl.ds(first + 16, 16), :] = pltpu.roll(rows, 64, 1)
+            return carry
+
+        lax.fori_loop(0, n, gather, 0)
+        beams = jnp.concatenate(
+            [turn[i * 128 : (i + 1) * 128, :].T[:64] for i in range(n * 32 // 128)], axis=1
+        )
+        baseline = jnp.sum(beams, axis=1, keepdims=True) / (n * 32)
+        out_ref[u] = beams / (baseline + eps_power)
+
     for u in range(TOUT):
+        if u >= 2:
+            finish(u - 2)
         each(volt_copy, "wait_recv", u)
         own_copy(u).wait()
 
@@ -319,23 +339,8 @@
     for u in range(TOUT):
         each(volt_copy, "wait_send", u)
 
-    for u in range(TOUT):
-        each(power_copy, "wait_recv", u)
-        own_power(u).wait()
-
-        def gather(src, carry, u=u):
-            rows = precv[u, src]
-            first = pl.multiple_of(src * 32, 32)
-            turn[pl.ds(first, 16), :] = rows
-            turn[pl.ds(first + 16, 16), :] = pltpu.roll(rows, 64, 1)
-            return carry
-
-        lax.fori_loop(0, n, gather, 0)
-        beams = jnp.concatenate(
-            [turn[i * 128 : (i + 1) * 128, :].T[:64] for i in range(n * 32 // 128)], axis=1
-        )
-        baseline = jnp.sum(beams, axis=1, keepdims=True) / (n * 32)
-        out_ref[u] = beams / (baseline + eps_power)
+    finish(TOUT - 2)
+    finish(TOUT - 1)
     for u in range(TOUT):
         each(power_copy, "wait_send", u)
 

time: 121 us -> 126 us (1.041)
  Pallas kernels: 118 us -> 124 us
    pallas_call x1, Pallas kernels: 118 us -> 124 us  [fused(): pl.pallas_call(functools.partial(beam_kernel, n), out_shape=jax.ShapeDtyp...]
where the time goes in v5:
time: 126 us
  Pallas kernels  124 us (98%)
  local copies, waits for them, and re-layouts  2.17 us (2%)
    pallas_call x1, Pallas kernels, fused(): pl.pallas_call(functools.partial(beam_kernel, n), out_shape=jax.ShapeDtyp...  124 us

profile of v5, /device:TPU:0, one launch (start us, length us, event | category | flops | bytes accessed | tf_op | source)
XLA Modules:
  0.0 125.7 jit_solution(18036811952879389337)
XLA Ops:
  0.0 123.6 %shard_map.64 = f32[4,64,512]{2,1,0:T(8,128)} custom-call(bf16[2,64,2,32,256]{4,3,2,1,0:T(8,128)(2,1)} %volt_ref.1, f32[2,2,64]{2,1,0:T(2,128)} %gain_ref.1, s32[8,128]{1,0:T(8,128)} %bitcast.5, s32[8,128]{1,0:T(8,128)} %bitcast.6, s32[4,4]{1,0:T(4,128)} %ew_ref.1, s32[2,128]{1,0:T(2,128)} %bitcast.7), custom_call_target="tpu_custom_call" | custom-call | tf_op jit(solution)/shard_map/pallas_call | solution.py:351
  123.6 2.2 %copy.7 = f32[64,4,512]{2,1,0:T(4,128)} copy(f32[64,4,512]{2,0,1:T(8,128)} %bitcast.4) | data formatting | bytes 1048576 | tf_op jit(solution)/shard_map/transpose | solution.py:386

commit v6 on v4

--- a/solution.py
+++ b/solution.py
@@ -204,7 +204,7 @@
         lax.fori_loop(1, n, one, 0)
 
     def produce(i, carry):
-        s = lax.rem(i + n // 2, n)
+        s = lax.rem(i + 1, n)
         d = lax.rem(me + s, n)
         for p in range(2):
             for c in range(2):

time: 121 us -> 123 us (1.017)
  Pallas kernels: 118 us -> 120 us
    pallas_call x1, Pallas kernels: 118 us -> 120 us  [fused(): pl.pallas_call(functools.partial(beam_kernel, n), out_shape=jax.ShapeDtyp...]
where the time goes in v6:
time: 123 us
  Pallas kernels  120 us (98%)
  local copies, waits for them, and re-layouts  2.17 us (2%)
    pallas_call x1, Pallas kernels, fused(): pl.pallas_call(functools.partial(beam_kernel, n), out_shape=jax.ShapeDtyp...  120 us

profile of v6, /device:TPU:0, one launch (start us, length us, event | category | flops | bytes accessed | tf_op | source)
XLA Modules:
  0.0 122.7 jit_solution(14549511087279183076)
XLA Ops:
  0.0 120.5 %shard_map.64 = f32[4,64,512]{2,1,0:T(8,128)} custom-call(bf16[2,64,2,32,256]{4,3,2,1,0:T(8,128)(2,1)} %volt_ref.1, f32[2,2,64]{2,1,0:T(2,128)} %gain_ref.1, s32[8,128]{1,0:T(8,128)} %bitcast.5, s32[8,128]{1,0:T(8,128)} %bitcast.6, s32[4,4]{1,0:T(4,128)} %ew_ref.1, s32[2,128]{1,0:T(2,128)} %bitcast.7), custom_call_target="tpu_custom_call" | custom-call | tf_op jit(solution)/shard_map/pallas_call | solution.py:346
  120.5 2.2 %copy.7 = f32[64,4,512]{2,1,0:T(4,128)} copy(f32[64,4,512]{2,0,1:T(8,128)} %bitcast.4) | data formatting | bytes 1048576 | tf_op jit(solution)/shard_map/transpose | solution.py:381
